TPU v7x, 32 devices: a whole 2x2x4 slice. The times are simulated.
32 devices in a mesh: ctx: 16 (over z, y, core), tp: 2 (over x).
Axes of the slice: x: 2, y: 2, z: 4, core: 2. Of those that a mesh axis runs over, the one named last changes fastest.
Arguments:
- tokens: bfloat16 [4096, 1024], P('ctx'), may hold values from -6 to 6
- seq_ids: int32 [4096], P('ctx'), may hold values from 0 to 3, never falling along the last dimension, each value on 1 to 2048 neighbouring positions
- attention_norm_gain: float32 [1024], replicated, may hold values from 0.5 to 1.5
- qkv_weight: bfloat16 [1024, 3, 1024], P(None, None, 'tp'), may hold values from -1 to 1, as said below
- out_weight: bfloat16 [1024, 1024], P('tp'), may hold values from -1.5 to 1.5
- feedforward_norm_gain: float32 [1024], replicated, may hold values from 0.5 to 1.5
- mlp_in_weight: bfloat16 [1024, 2, 2624], P(None, None, 'tp'), may hold values from -0.1875 to 0.1875
- mlp_out_weight: bfloat16 [2624, 1024], P('tp'), may hold values from -0.125 to 0.125
- grad_out: bfloat16 [4096, 1024], P('ctx'), may hold values from -6 to 6
Outputs:
- output: bfloat16 [4096, 1024], P('ctx')
- grad_tokens: float32 [4096, 1024], P('ctx')
- grad_norm1_gain: float32 [1024], replicated
- grad_qkv_weight: float32 [1024, 3, 1024], P(None, None, 'tp')
- grad_out_weight: float32 [1024, 1024], P('tp')
- grad_norm2_gain: float32 [1024], replicated
- grad_mlp_in_weight: float32 [1024, 2, 2624], P(None, None, 'tp')
- grad_mlp_out_weight: float32 [2624, 1024], P('tp')
Inputs may be any that keep to these rules, and one draw needn't show every extreme that they name: `seq_ids`: never falling along the tokens; every one of the 4 sequences has at least one token and one has exactly 2048. `qkv_weight`: A projection matrix with entries of order 1024^(-1/2).
All inputs are finite; a program needn't handle non-finite values.
Results may differ from a plain program's by a relative error of at most 0.025.
Values may be sent and summed in bfloat16 or wider, within the bound.
No kernel may reach another device: no remote copies, remote signals or barrier semaphores. Data moves between devices by JAX's collectives and lax.ppermute only.
A program may use at most 256 MiB of HBM per device.

v0:
```python
import math

import jax
import jax.numpy as jnp
from jax import lax
from jax.sharding import PartitionSpec as P

HD = 64


EPS = 1e-05
BASE = 160000.0
MASKED = -1e30
ROOT_HALF = 0.7071067811865476
INV_ROOT_TWO_PI = 0.3989422804014327


def layer_normalize(values_in, norm_gain_vector):
    token_average = jnp.mean(values_in, axis=-1, keepdims=True)
    centered_input = values_in - token_average
    inverse_deviation = lax.rsqrt(
        jnp.mean(centered_input * centered_input, axis=-1, keepdims=True) + EPS
    )
    standardized_input = centered_input * inverse_deviation
    return (standardized_input, inverse_deviation, standardized_input * norm_gain_vector)


def layer_normalize_backward(
    output_gradient, standardized_input, inverse_deviation, norm_gain_vector
):
    normalized_gradient = output_gradient * norm_gain_vector
    correction_term = jnp.mean(
        normalized_gradient, axis=-1, keepdims=True
    ) + standardized_input * jnp.mean(
        normalized_gradient * standardized_input, axis=-1, keepdims=True
    )
    return (
        inverse_deviation * (normalized_gradient - correction_term),
        jnp.sum(output_gradient * standardized_input, axis=0),
    )


def gelu_value(v):
    return v * 0.5 * (1.0 + lax.erf(v * ROOT_HALF))


def gelu_slope(v):
    return 0.5 * (1.0 + lax.erf(v * ROOT_HALF)) + v * jnp.exp(-0.5 * v * v) * INV_ROOT_TWO_PI


def rope_tables(positions, head_size):
    half = head_size // 2
    inverse = BASE ** (-(jnp.arange(half, dtype=jnp.float32) * (2.0 / head_size)))
    angle = positions.astype(jnp.float32)[:, None] * inverse[None, :]
    angle = jnp.concatenate([angle, angle], axis=-1)
    return (jnp.cos(angle), jnp.sin(angle))


def rotate(field, cosine, sine):
    half = field.shape[-1] // 2
    turned = jnp.concatenate([-field[..., half:], field[..., :half]], axis=-1)
    return field * cosine[:, None, :] + turned * sine[:, None, :]


def unrotate(grad, cosine, sine):
    half = grad.shape[-1] // 2
    lifted = grad * sine[:, None, :]
    back = jnp.concatenate([lifted[..., half:], -lifted[..., :half]], axis=-1)
    return grad * cosine[:, None, :] + back


def block_grads(q_rows, do_rows, lse_rows, delta_rows, seq_rows, k_rows, v_rows, seq_cols, scale):
    f32 = jnp.float32
    scores = jnp.einsum("qhd,khd->hqk", q_rows, k_rows, preferred_element_type=f32) * scale
    same = (seq_rows[:, None] == seq_cols[None, :])[None]
    probs = jnp.where(same, jnp.exp(scores - lse_rows.T[:, :, None]), 0.0)
    grad_v = jnp.einsum(
        "hqk,qhd->khd", probs.astype(jnp.bfloat16), do_rows, preferred_element_type=f32
    )
    grad_p = jnp.einsum("qhd,khd->hqk", do_rows, v_rows, preferred_element_type=f32)
    grad_s = (probs * (grad_p - delta_rows.T[:, :, None])).astype(jnp.bfloat16)
    grad_q = jnp.einsum("hqk,khd->qhd", grad_s, k_rows, preferred_element_type=f32) * scale
    grad_k = jnp.einsum("hqk,qhd->khd", grad_s, q_rows, preferred_element_type=f32) * scale
    return (grad_q, grad_k, grad_v)


def per_device(
    tokens,
    seq_ids,
    attention_norm_gain,
    qkv_weight,
    out_weight,
    feedforward_norm_gain,
    mlp_in_weight,
    mlp_out_weight,
    grad_out,
):
    f32 = jnp.float32
    bf16 = jnp.bfloat16
    tok_rows, width = tokens.shape
    local_cols = qkv_weight.shape[2]
    heads_here = local_cols // HD
    hidden_here = mlp_in_weight.shape[2]
    scale = 1.0 / math.sqrt(HD)
    input_tokens = tokens.astype(f32)
    attention_standardized, attention_inverse_deviation, attention_normed_input = layer_normalize(
        input_tokens, attention_norm_gain
    )
    first = attention_normed_input.astype(bf16)
    qkv_flat = qkv_weight.reshape(width, 3 * local_cols)
    proj = jnp.dot(first, qkv_flat, preferred_element_type=f32).reshape(tok_rows, 3, heads_here, HD)
    positions = lax.axis_index("ctx") * tok_rows + jnp.arange(tok_rows, dtype=jnp.int32)
    cosine, sine = rope_tables(positions, HD)
    query = rotate(proj[:, 0], cosine, sine).astype(bf16)
    keys = rotate(proj[:, 1], cosine, sine).astype(bf16)
    values = proj[:, 2].astype(bf16)
    keys_flat = keys.reshape(tok_rows, local_cols)
    values_flat = values.reshape(tok_rows, local_cols)
    run_max = jnp.full((heads_here, tok_rows), MASKED, f32)
    key_piece = lax.all_gather(keys_flat, "ctx", axis=0, tiled=True)
    value_piece = lax.all_gather(values_flat, "ctx", axis=0, tiled=True)
    seq_piece = lax.all_gather(seq_ids, "ctx", axis=0, tiled=True)
    count = key_piece.shape[0]
    key_heads = key_piece.reshape(count, heads_here, HD)
    value_heads = value_piece.reshape(count, heads_here, HD)
    scores = jnp.einsum("qhd,khd->hqk", query, key_heads, preferred_element_type=f32) * scale
    same = (seq_ids[:, None] == seq_piece[None, :])[None]
    top = jnp.max(jnp.where(same, scores, MASKED), axis=-1)
    new_max = jnp.maximum(run_max, top)
    weights = jnp.where(same, jnp.exp(scores - new_max[..., None]), 0.0)
    run_sum = jnp.sum(weights, axis=-1)
    added = jnp.einsum(
        "hqk,khd->hqd", weights.astype(bf16), value_heads, preferred_element_type=f32
    )
    run_acc = added
    run_max, run_sum, run_acc = (new_max, run_sum, run_acc)
    attended = (run_acc / run_sum[..., None]).transpose(1, 0, 2).astype(bf16)
    lse = (run_max + jnp.log(run_sum)).T
    attended_flat = attended.reshape(tok_rows, local_cols)
    attn_part = jnp.dot(attended_flat, out_weight, preferred_element_type=f32)
    residual_middle = input_tokens + lax.psum(attn_part.astype(jnp.bfloat16), "tp").astype(
        jnp.float32
    )
    feedforward_standardized, feedforward_inverse_deviation, feedforward_normed_input = (
        layer_normalize(residual_middle, feedforward_norm_gain)
    )
    second = feedforward_normed_input.astype(bf16)
    in_flat = mlp_in_weight.reshape(width, 2 * hidden_here)
    mixed = jnp.dot(second, in_flat, preferred_element_type=f32).reshape(tok_rows, 2, hidden_here)
    act_in = mixed[:, 0]
    gate = mixed[:, 1]
    hidden = (gelu_value(act_in) * gate).astype(bf16)
    ffn_part = jnp.dot(hidden, mlp_out_weight, preferred_element_type=f32)
    output = (
        residual_middle + lax.psum(ffn_part.astype(jnp.bfloat16), "tp").astype(jnp.float32)
    ).astype(bf16)
    upstream = grad_out.astype(f32)
    grad_w_out = jnp.dot(hidden.T, grad_out, preferred_element_type=f32)
    grad_hidden = jnp.dot(grad_out, mlp_out_weight.T, preferred_element_type=f32)
    grad_mixed = jnp.stack(
        [grad_hidden * gate * gelu_slope(act_in), grad_hidden * gelu_value(act_in)], axis=1
    ).astype(bf16)
    grad_mixed_flat = grad_mixed.reshape(tok_rows, 2 * hidden_here)
    grad_w_in = jnp.dot(second.T, grad_mixed_flat, preferred_element_type=f32).reshape(
        width, 2, hidden_here
    )
    second_part = jnp.dot(grad_mixed_flat, in_flat.T, preferred_element_type=f32)
    feedforward_norm_gradient = lax.psum(second_part.astype(jnp.bfloat16), "tp").astype(jnp.float32)
    feedforward_normed_gradient, feedforward_gain_gradient = layer_normalize_backward(
        feedforward_norm_gradient,
        feedforward_standardized,
        feedforward_inverse_deviation,
        feedforward_norm_gain,
    )
    grad_mid = upstream + feedforward_normed_gradient
    grad_mid_b = grad_mid.astype(bf16)
    grad_w_attn = jnp.dot(attended_flat.T, grad_mid_b, preferred_element_type=f32)
    grad_att = (
        jnp.dot(grad_mid_b, out_weight.T, preferred_element_type=f32)
        .astype(bf16)
        .reshape(tok_rows, heads_here, HD)
    )
    delta = jnp.sum(grad_att.astype(f32) * attended.astype(f32), axis=-1)
    key_piece = lax.all_gather(keys_flat, "ctx", axis=0, tiled=True)
    value_piece = lax.all_gather(values_flat, "ctx", axis=0, tiled=True)
    seq_piece = lax.all_gather(seq_ids, "ctx", axis=0, tiled=True)
    count = key_piece.shape[0]
    key_heads = key_piece.reshape(count, heads_here, HD)
    value_heads = value_piece.reshape(count, heads_here, HD)
    gq, gk, gv = block_grads(
        query, grad_att, lse, delta, seq_ids, key_heads, value_heads, seq_piece, scale
    )
    pair = jnp.stack([gk.reshape(count, local_cols), gv.reshape(count, local_cols)], axis=1)
    own_pairs = lax.psum_scatter(
        pair.astype(jnp.bfloat16), "ctx", scatter_dimension=0, tiled=True
    ).astype(jnp.float32)
    grad_key = own_pairs[:, 0].reshape(tok_rows, heads_here, HD)
    grad_value = own_pairs[:, 1].reshape(tok_rows, heads_here, HD)
    grad_proj = jnp.stack(
        [unrotate(gq, cosine, sine), unrotate(grad_key, cosine, sine), grad_value], axis=1
    )
    grad_proj = grad_proj.astype(bf16).reshape(tok_rows, 3 * local_cols)
    grad_w_qkv = jnp.dot(first.T, grad_proj, preferred_element_type=f32).reshape(
        width, 3, local_cols
    )
    first_part = jnp.dot(grad_proj, qkv_flat.T, preferred_element_type=f32)
    attention_norm_gradient = lax.psum(first_part.astype(jnp.bfloat16), "tp").astype(jnp.float32)
    attention_normed_gradient, attention_gain_gradient = layer_normalize_backward(
        attention_norm_gradient,
        attention_standardized,
        attention_inverse_deviation,
        attention_norm_gain,
    )
    grad_tokens = grad_mid + attention_normed_gradient
    summed = (
        lax.psum(attention_gain_gradient.astype(jnp.bfloat16), "ctx").astype(jnp.float32),
        lax.psum(grad_w_qkv.astype(jnp.bfloat16), "ctx").astype(jnp.float32),
        lax.psum(grad_w_attn.astype(jnp.bfloat16), "ctx").astype(jnp.float32),
        lax.psum(feedforward_gain_gradient.astype(jnp.bfloat16), "ctx").astype(jnp.float32),
        lax.psum(grad_w_in.astype(jnp.bfloat16), "ctx").astype(jnp.float32),
        lax.psum(grad_w_out.astype(jnp.bfloat16), "ctx").astype(jnp.float32),
    )
    return (output, grad_tokens, summed[0], summed[1], summed[2], summed[3], summed[4], summed[5])


def solution(mesh):
    return jax.shard_map(
        per_device,
        mesh=mesh,
        in_specs=(
            P("ctx", None),
            P("ctx"),
            P(),
            P(None, None, "tp"),
            P("tp", None),
            P(),
            P(None, None, "tp"),
            P("tp", None),
            P("ctx", None),
        ),
        out_specs=(
            P("ctx", None),
            P("ctx", None),
            P(),
            P(None, None, "tp"),
            P("tp", None),
            P(),
            P(None, None, "tp"),
            P("tp", None),
        ),
        check_vma=False,
    )
```

profile of v0, /device:TPU:0, one launch (start us, length us, event | category | flops | bytes accessed | tf_op | source)
XLA Modules:
  0.0 697.5 jit_solution(1876158596142752087)
XLA Ops:
  7.3 4.8 copy.22
  12.6 3.0 fusion.57
  16.8 1.2 fusion.76
  18.9 1.3 slice_negate_fusion.2
  20.2 1.2 maximum_multiply_fusion.1
  22.3 1.8 slice.110
  24.1 23.5 %all-gather = s32[16,1,256]{2,1,0:T(1,128)S(1)} all-gather(s32[1,1,256]{2,1,0:T(1,128)S(1)} %bitcast.163), channel_id=1, replica_groups=mesh['ctx'=16,'tp'=2] {'ctx'}, dimensions={0}, use_global_device_ids=true | all-gather | bytes 17408 | tf_op jit(solution)/shard_map/all_gather | solution.py:122
  47.6 1.6 broadcast_compare_fusion
  49.2 28.3 %all-gather.4.cloned.1.call-done = bf16[4096,512]{0,1:T(8,128)(2,1)} async-done(((bf16[256,512]{0,1:T(8,128)(2,1)}), bf16[4096,512]{0,1:T(8,128)(2,1)}) %all-gather.4.cloned.1.call-update) | async-done | bytes 4194320 | tf_op jit(solution)/shard_map/all_gather | solution.py:120
  77.5 16.5 %select_reduce_fusion = (f32[8,256]{1,0:T(8,128)S(1)}, f32[8,256,4096]{2,1,0:T(8,128)}) fusion(pred[256,4096]{1,0:T(8,128)(4,1)} %broadcast_compare_fusion, bf16[256,8,64]{0,2,1:T(8,128)(2,1)S(1)} %get-tuple-element.38, bf16[4096,8,64]{0,2,1:T(8,128)(2,1)} %bitcast.142), kind=kOutput, calls=%fused_computation.3 | convolution fusion | flops 1098905600 | bytes 39067648 | tf_op jit(solution)/shard_map/qhd,khd->hqk/dot_general | solution.py:126
  94.6 16.2 %fusion = f32[8,256]{1,0:T(8,128)} fusion(f32[8,256,4096]{2,1,0:T(8,128)} %get-tuple-element.44, f32[8,256]{1,0:T(8,128)S(1)} %broadcast_maximum_fusion, pred[256,4096]{1,0:T(8,128)(4,1)S(1)} %copy-done.4), kind=kLoop, calls=%fused_computation.4 | loop fusion | flops 33552384 | bytes 34619392 | tf_op jit(solution)/shard_map/reduce_sum | solution.py:131
  110.8 20.1 %all-gather.6.cloned.1.call-done = bf16[4096,512]{0,1:T(8,128)(2,1)} async-done(((bf16[256,512]{0,1:T(8,128)(2,1)}), bf16[4096,512]{0,1:T(8,128)(2,1)}) %all-gather.6.cloned.1.call-update) | async-done | bytes 4194320 | tf_op jit(solution)/shard_map/all_gather | solution.py:121
  130.9 16.3 %fusion.49 = bf16[256,8,64]{0,2,1:T(8,128)(2,1)} fusion(bf16[4096,8,64]{0,2,1:T(8,128)(2,1)} %bitcast.164, f32[8,256,4096]{2,1,0:T(8,128)} %get-tuple-element.44, f32[8,256]{1,0:T(8,128)} %copy-done.29, pred[256,4096]{1,0:T(8,128)(4,1)} %broadcast_compare_fusion, f32[256,8]{0,1:T(8,128)} %bitcast.161), kind=kOutput, calls=%fused_computation.78 | convolution fusion | flops 1107558400 | bytes 39075840 | tf_op jit(solution)/shard_map/hqk,khd->hqd/dot_general | solution.py:132
  147.2 2.6 convolution_convert_fusion.4
  150.0 26.8 %all-reduce.8.cloned.1.call-done = bf16[256,1024]{1,0:T(8,128)(2,1)} async-done(((bf16[256,1024]{1,0:T(8,128)(2,1)}), bf16[256,1024]{1,0:T(8,128)(2,1)}) %all-reduce.8.cloned.1.call-update) | async-done | bytes 524304 | tf_op jit(solution)/shard_map/psum | solution.py:141
  176.8 1.3 fusion.52
  178.1 1.3 multiply_reduce_fusion
  179.4 4.5 fusion.12
  184.0 1.4 fusion.19
  186.6 5.0 fusion.27
  191.7 1.3 log_add_fusion
  193.0 27.5 %all-reduce.10.cloned.1.call-done = bf16[256,1024]{1,0:T(8,128)(2,1)} async-done(((bf16[256,1024]{1,0:T(8,128)(2,1)}), bf16[256,1024]{1,0:T(8,128)(2,1)}) %all-reduce.10.cloned.1.call-update) | async-done | bytes 524304 | tf_op jit(solution)/shard_map/psum | solution.py:168
  220.5 2.5 fusion.41
  222.9 1.8 fusion.40
  225.8 1.2 convolution_convert_fusion.7
  226.9 1.8 copy.23
  229.8 19.3 %fusion.9 = bf16[8,64,4096]{2,1,0:T(8,128)(2,1)} fusion(bf16[256,8,64]{0,2,1:T(8,128)(2,1)} %bitcast.158, f32[8,256,4096]{2,1,0:T(8,128)} %get-tuple-element.44, f32[8,256]{1,0:T(8,128)} %log_add_fusion, pred[256,4096]{1,0:T(8,128)(4,1)} %broadcast_compare_fusion), kind=kOutput, calls=%fused_computation.13 | convolution fusion | flops 1109393408 | bytes 39067648 | tf_op jit(solution)/shard_map/hqk,qhd->khd/dot_general | solution.py:77
  249.2 23.4 %multiply_convert_fusion = bf16[8,256,4096]{2,1,0:T(8,128)(2,1)} fusion(f32[8,256,4096]{2,1,0:T(8,128)} %get-tuple-element.44, f32[8,256]{1,0:T(8,128)S(1)} %bitcast.162, f32[8,256]{1,0:T(8,128)} %log_add_fusion, pred[256,4096]{1,0:T(8,128)(4,1)} %broadcast_compare_fusion, bf16[256,8,64]{0,2,1:T(8,128)(2,1)} %bitcast.159, bf16[4096,8,64]{0,2,1:T(8,128)(2,1)} %bitcast.165), kind=kOutput, calls=%fused_computation | convolution fusion | flops 1124073472 | bytes 55853056 | tf_op jit(solution)/shard_map/qhd,khd->hqk/dot_general | solution.py:80
  272.6 10.8 %multiply_convert_fusion.1 = bf16[8,64,4096]{2,1,0:T(8,128)(2,1)} fusion(bf16[256,8,64]{0,2,1:T(8,128)(2,1)S(1)} %get-tuple-element.38, bf16[8,256,4096]{2,1,0:T(8,128)(2,1)} %multiply_convert_fusion), kind=kOutput, calls=%fused_computation.12 | convolution fusion | flops 1077936128 | bytes 21233664 | tf_op jit(solution)/shard_map/hqk,qhd->khd/dot_general | solution.py:83
  283.4 7.6 %pad_maximum_fusion = bf16[4096,2,512]{0,2,1:T(8,128)(2,1)} fusion(bf16[4096,1,512]{0,2,1:T(8,128)(2,1)} %bitcast.149, bf16[4096,1,512]{0,2,1:T(8,128)(2,1)} %bitcast.144), kind=kLoop, calls=%fused_computation.11 | loop fusion | flops 4194304 | bytes 16777216 | tf_op jit(solution)/shard_map/stack | solution.py:193
  291.4 2.0 multiply_convert_fusion.2
  294.3 1.8 convolution_convert_fusion.5
  296.1 15.0 %broadcast_multiply_fusion = (f32[256,8,64]{0,2,1:T(8,128)}, f32[256,8,64]{0,2,1:T(8,128)}) fusion(f32[256,64]{0,1:T(8,128)S(1)} %copy-done.22, bf16[4096,8,64]{0,2,1:T(8,128)(2,1)} %bitcast.143, bf16[8,256,4096]{2,1,0:T(8,128)(2,1)} %multiply_convert_fusion), kind=kOutput, calls=%fused_computation.103 | convolution fusion | flops 1073872896 | bytes 22085632 | tf_op jit(solution)/shard_map/hqk,khd->qhd/dot_general | solution.py:82
  313.4 81.5 %reduce-scatter.2.cloned.1.call-done = bf16[256,2,512]{0,2,1:T(8,128)(2,1)} async-done(((bf16[4096,2,512]{0,2,1:T(8,128)(2,1)}), bf16[256,2,512]{0,2,1:T(8,128)(2,1)}) %reduce-scatter.2.cloned.1.call-update) | async-done | bytes 524304 | tf_op jit(solution)/shard_map/reduce_scatter | solution.py:194
  398.0 1.8 convolution_convert_fusion.6
  399.9 3.8 convolution_convert_fusion.1
  403.8 4.2 convolution_convert_fusion
  407.9 1.4 convolution_convert_fusion.3
  409.4 2.9 convolution_convert_fusion.2
  412.3 27.5 %all-reduce.14.cloned.1.call-done = (bf16[256,1024]{1,0:T(8,128)(2,1)}, bf16[256,1024]{1,0:T(8,128)(2,1)}) async-done(((bf16[256,1024]{1,0:T(8,128)(2,1)}, bf16[256,1024]{1,0:T(8,128)(2,1)}), (bf16[256,1024]{1,0:T(8,128)(2,1)}, bf16[256,1024]{1,0:T(8,128)(2,1)})) %all-reduce.14.cloned.1.call-update) | async-done | bytes 1048592 | tf_op jit(solution)/shard_map/psum | solution.py:155
  439.7 1.6 fusion.45
  441.3 34.7 %all-reduce = (bf16[1024]{0:T(1024)(128)(2,1)S(1)}, bf16[1024]{0:T(1024)(128)(2,1)S(1)}) all-reduce(bf16[1024]{0:T(1024)(128)(2,1)S(1)} %get-tuple-element.10, bf16[1024]{0:T(1024)(128)(2,1)S(1)} %copy-done.34), channel_id=1, replica_groups=mesh['ctx'=16,'tp'=2] {'ctx'}, use_global_device_ids=true, to_apply=%region_17.18 | all-reduce | flops 2048 | bytes 8192 | tf_op jit(solution)/shard_map/psum | solution.py:216
  477.3 3.3 fusion.44
  480.6 193.8 %all-reduce.12.cloned.1.call-done = (bf16[1024,3,512]{2,0,1:T(8,128)(2,1)}, bf16[512,1024]{1,0:T(8,128)(2,1)}, bf16[1024,2,1312]{0,2,1:T(8,128)(2,1)}, bf16[1312,1024]{1,0:T(8,128)(2,1)}) async-done(((bf16[1024,3,512]{2,0,1:T(8,128)(2,1)}, bf16[512,1024]{1,0:T(8,128)(2,1)}, bf16[1024,2,1312]{0,2,1:T(8,128)(2,1)}, bf16[1312,1024]{1,0:T(8,128)(2,1)}), (bf16[1024,3,512]{2,0,1:T(8,128)(2,1)}, ...) | async-done | bytes 12255248 | tf_op jit(solution)/shard_map/psum | solution.py:217
  674.4 5.6 convert_element_type.179
  680.0 1.6 convert_element_type.181
  681.6 5.5 convert_element_type.186
  687.1 3.1 convert_element_type.188
  (119 shorter events, 15.5 us)
Async XLA Ops:
  7.2 176.8 %copy-start = (bf16[1312,1024]{1,0:T(8,128)(2,1)S(1)}, bf16[1312,1024]{1,0:T(8,128)(2,1)}, u32[]{:S(2)}) copy-start(bf16[1312,1024]{1,0:T(8,128)(2,1)} %param.16) | copy-start | bytes 8060932
  7.2 4.9 copy-start.1
  7.2 5.4 copy-start.25
  7.2 70.3 %all-gather.4.cloned.1.call-start = ((), (), s32[]{:S(2)}) async-start(), calls=%async_computation.1 | async-start | bytes 4456448 | tf_op jit(solution)/shard_map/all_gather | solution.py:120
  12.2 3.4 copy-start.30
  12.5 3.1 copy-start.32
  15.6 1.1 copy-start.14
  18.0 6.1 copy-start.35
  18.0 3.4 copy-start.15
  18.9 2.5 copy-start.23
  22.2 108.7 %all-gather.6.cloned.1.call-start = ((), (), s32[]{:S(2)}) async-start(), calls=%async_computation.2 | async-start | bytes 4456448 | tf_op jit(solution)/shard_map/all_gather | solution.py:121
  24.1 152.7 %all-reduce.8.cloned.1.call-start = ((), (), s32[]{:S(2)}) async-start(), calls=%async_computation.3 | async-start | bytes 1048576 | tf_op jit(solution)/shard_map/psum | solution.py:141
  77.5 17.1 %copy-start.4 = (pred[256,4096]{1,0:T(8,128)(4,1)S(1)}, pred[256,4096]{1,0:T(8,128)(4,1)}, u32[]{:S(2)}) copy-start(pred[256,4096]{1,0:T(8,128)(4,1)} %broadcast_compare_fusion) | copy-start | bytes 3145732
  94.0 0.6 copy-start.29
  147.2 32.2 %copy-start.24 = (f32[1024]{0:T(1024)S(1)}, f32[1024]{0:T(1024)}, u32[]{:S(2)}) copy-start(f32[1024]{0:T(1024)} %param.14) | copy-start | bytes 12292
  149.8 70.6 %all-reduce.10.cloned.1.call-start = ((), (), s32[]{:S(2)}) async-start(), calls=%async_computation.4 | async-start | bytes 1048576 | tf_op jit(solution)/shard_map/psum | solution.py:168
  179.4 4.5 copy-start.27
  179.4 4.5 copy-start.16
  184.0 1.6 copy-start.3
  185.5 0.8 copy-start.18
  185.5 1.1 copy-start.20
  191.6 203.2 %reduce-scatter.2.cloned.1.call-start = ((), (), s32[]{:S(2)}) async-start(), calls=%async_computation.5 | async-start | bytes 8912896 | tf_op jit(solution)/shard_map/reduce_scatter | solution.py:194
  220.5 5.3 copy-start.8
  224.8 1.0 copy-start.5
  291.1 5.0 copy-start.22
  291.1 148.6 %all-reduce.14.cloned.1.call-start = ((), (), s32[]{:S(2)}) async-start(), calls=%async_computation.7 | async-start | bytes 2097152 | tf_op jit(solution)/shard_map/psum | solution.py:155
  293.4 0.8 copy-start.7
  394.8 2.2 slice-start.2
  394.8 3.2 copy-start.11
  397.1 0.9 copy-start.9
  399.8 3.9 copy-start.28
  399.8 274.5 %all-reduce.12.cloned.1.call-start = ((), (), s32[]{:S(2)}) async-start(), calls=%async_computation.6 | async-start | bytes 24510464 | tf_op jit(solution)/shard_map/psum | solution.py:217
  399.9 3.8 copy-start.2
  399.9 3.8 copy-start.19
  399.9 3.8 copy-start.21
  403.7 4.2 copy-start.6
  403.7 4.2 copy-start.13
  403.7 5.6 copy-start.10
  403.7 5.6 copy-start.26
  403.7 5.6 copy-start.31
  403.8 5.6 copy-start.33
  412.2 29.1 %copy-start.34 = (bf16[1024]{0:T(1024)(128)(2,1)S(1)}, bf16[1024]{0:T(1024)(128)(2,1)}, u32[]{:S(2)}) copy-start(bf16[1024]{0:T(1024)(128)(2,1)} %get-tuple-element.8) | copy-start | bytes 6148
  674.4 7.2 %slice-start = ((s8[5373952]{0:T(1024)(128)(4,1)}), s8[4194304]{0:T(1024)(128)(4,1)S(1)}, s32[]{:S(2)}) async-start(s8[5373952]{0:T(1024)(128)(4,1)} %bitcast.145), calls=%async_computation.8 | async-start | bytes 8388608
  674.4 5.7 copy-start.17
  674.4 7.2 %slice-start.1 = ((s8[5373952]{0:T(1024)(128)(4,1)}), s8[1179648]{0:T(1024)(128)(4,1)S(1)}, s32[]{:S(2)}) async-start(s8[5373952]{0:T(1024)(128)(4,1)} %bitcast.145), calls=%async_computation.9 | async-start | bytes 2359296
  681.6 5.5 copy-start.12
Sparse Core Ops, SparseCore 0:
  22.3 55.1 all-gather.3
  80.2 50.6 all-gather.5
  149.9 26.8 all-reduce.7
  191.8 28.6 all-reduce.9
  291.2 103.5 reduce-scatter.1
  400.0 39.7 all-reduce.13
  445.0 229.3 all-reduce.11
where the time goes:
time: 706 us; the launch traced here: 697 us
  waiting for transfers between devices  405 us (57%)
  matrix products  135 us (19%)
  other arithmetic  66.6 us (9%)
  blocking collectives  58.2 us (8%)
  local copies, waits for them, and re-layouts  16.6 us (2%)
  between operations  15.1 us (2%)
    psum x1, waiting for transfers between devices, per_device(): lax.psum(grad_w_qkv.astype(jnp.bfloat16), 'ctx').astype(jnp.float32)  194 us
    reduce_scatter x1, waiting for transfers between devices, per_device(): lax.psum_scatter(pair.astype(jnp.bfloat16), 'ctx', scatter_dimension=0, t...  81.5 us
    psum x1, blocking collectives, per_device(): lax.psum(attention_gain_gradient.astype(jnp.bfloat16), 'ctx')  34.7 us
    all_gather x1, waiting for transfers between devices, per_device(): key_piece = lax.all_gather(keys_flat, 'ctx', axis=0, tiled=True)  28.3 us
    psum x1, waiting for transfers between devices, per_device(): lax.psum(ffn_part.astype(jnp.bfloat16), 'tp').astype(jnp.float32)  27.5 us
    psum x1, waiting for transfers between devices, per_device(): lax.psum(second_part.astype(jnp.bfloat16), 'tp').astype(jnp.float32)  27.5 us
    psum x1, waiting for transfers between devices, per_device(): lax.psum(attn_part.astype(jnp.bfloat16), 'tp').astype(jnp.float32)  26.8 us
    all_gather x1, blocking collectives, per_device(): seq_piece = lax.all_gather(seq_ids, 'ctx', axis=0, tiled=True)  23.5 us
  transfers between devices with their start and end apart: 7, of which 7 were waited for; matrix products, arithmetic and copies ran while one was open for 11% of the time, Pallas kernels for 0%

commit v1 on v0

v1 whole, which is shorter than its diff:
```python
import functools
import math

import jax
import jax.numpy as jnp
from jax import lax
from jax.experimental import pallas as pl
from jax.experimental.pallas import tpu as pltpu
from jax.sharding import PartitionSpec as P

HD = 64
EPS = 1e-05
BASE = 160000.0
MASKED = -1e30
ROOT_HALF = 0.7071067811865476
INV_ROOT_TWO_PI = 0.3989422804014327
SEQS = 4
F32 = jnp.float32
BF16 = jnp.bfloat16
PAD = 16


def layer_normalize(values_in, norm_gain_vector):
    token_average = jnp.mean(values_in, axis=-1, keepdims=True)
    centered_input = values_in - token_average
    inverse_deviation = lax.rsqrt(
        jnp.mean(centered_input * centered_input, axis=-1, keepdims=True) + EPS
    )
    standardized_input = centered_input * inverse_deviation
    return (standardized_input, inverse_deviation, standardized_input * norm_gain_vector)


def layer_normalize_backward(
    output_gradient, standardized_input, inverse_deviation, norm_gain_vector
):
    normalized_gradient = output_gradient * norm_gain_vector
    correction_term = jnp.mean(
        normalized_gradient, axis=-1, keepdims=True
    ) + standardized_input * jnp.mean(
        normalized_gradient * standardized_input, axis=-1, keepdims=True
    )
    return (
        inverse_deviation * (normalized_gradient - correction_term),
        jnp.sum(output_gradient * standardized_input, axis=0),
    )


def gelu_value(v):
    return v * 0.5 * (1.0 + lax.erf(v * ROOT_HALF))


def gelu_slope(v):
    return 0.5 * (1.0 + lax.erf(v * ROOT_HALF)) + v * jnp.exp(-0.5 * v * v) * INV_ROOT_TWO_PI


def rope_tables_t(positions, head_size):
    half = head_size // 2
    inverse = BASE ** (-(jnp.arange(half, dtype=F32) * (2.0 / head_size)))
    angle = inverse[:, None] * positions.astype(F32)[None, :]
    return (jnp.cos(angle), jnp.sin(angle))


def rotate_t(field, cosine, sine):
    half = field.shape[1] // 2
    one, two = field[:, :half], field[:, half:]
    return jnp.concatenate([one * cosine - two * sine, two * cosine + one * sine], axis=1)


def unrotate_t(grad, cosine, sine):
    half = grad.shape[1] // 2
    one, two = grad[:, :half], grad[:, half:]
    return jnp.concatenate([one * cosine + two * sine, two * cosine - one * sine], axis=1)


def fill_natural(kvn, own, oth, groups, count, chunk):
    for r in range(groups):
        for c in range(count // chunk):
            at = slice(c * chunk, (c + 1) * chunk)
            if r == 0:
                piece = own[HD : 3 * HD, at]
            else:
                piece = oth[r - 1, 0 : 2 * HD, at]
            kvn[r * count + c * chunk : r * count + (c + 1) * chunk, :] = (
                piece.astype(F32).T.astype(BF16)
            )


def forward_kernel(lo, hi, q_ref, own, oth, rows, out, lse, kvn, *, groups, count, kb):
    i = pl.program_id(0)

    @pl.when(i == 0)
    def _():
        fill_natural(kvn, own, oth, groups, count, min(count, 256))

    qb = q_ref.shape[1]
    q = (q_ref[...].astype(F32) * (1.0 / math.sqrt(HD))).astype(BF16)
    q = jnp.concatenate([q, jnp.zeros_like(q)], axis=0)
    spot = lax.broadcasted_iota(jnp.int32, (kb, qb), 0)
    carry = (
        jnp.full((1, qb), MASKED, F32),
        jnp.zeros((1, qb), F32),
        jnp.zeros((HD, qb), F32),
    )
    for r in range(groups):
        first = rows[r : r + 1, :]
        end = rows[groups + r : groups + r + 1, :]

        def step(j, carry, r=r, first=first, end=end):
            top, den, acc = carry
            k0 = pl.multiple_of(j * kb, kb)
            s = jnp.dot(kvn[pl.ds(r * count + k0, kb), :], q, preferred_element_type=F32)
            s = jnp.where((spot >= first - k0) & (spot < end - k0), s, MASKED)
            new = jnp.maximum(top, jnp.max(s, axis=0, keepdims=True))
            p = jnp.exp(s - new)
            fade = jnp.exp(top - new)
            den = den * fade + jnp.sum(p, axis=0, keepdims=True)
            if r == 0:
                v = own[2 * HD : 3 * HD, pl.ds(k0, kb)]
            else:
                v = oth[r - 1, HD : 2 * HD, pl.ds(k0, kb)]
            acc = acc * fade + jnp.dot(v, p.astype(BF16), preferred_element_type=F32)
            return (new, den, acc)

        carry = lax.fori_loop(
            lo[i * groups + r] // kb, (hi[i * groups + r] + kb - 1) // kb, step, carry
        )
    top, den, acc = carry
    out[...] = (acc / den).astype(BF16)
    lse[...] = top + jnp.log(den)


def backward_kernel(
    lo, hi, q_ref, own, oth, rows, out, do_ref, lse, dq, dkv, dkv_oth, kvn, acc,
    *, groups, count, kb
):
    i = pl.program_id(0)

    @pl.when(i == 0)
    def _():
        fill_natural(kvn, own, oth, groups, count, min(count, 256))
        acc[...] = jnp.zeros_like(acc)

    qb = q_ref.shape[1]
    scale = 1.0 / math.sqrt(HD)
    qf = q_ref[...].astype(F32) * scale
    q = qf.astype(BF16)
    do = do_ref[...]
    dof = do.astype(F32)
    delta = jnp.sum(dof * out[...].astype(F32), axis=0, keepdims=True)
    none = jnp.zeros_like(q)
    q_pad = jnp.concatenate([q, none], axis=0)
    do_pad = jnp.concatenate([none, do], axis=0)
    q_nat = jnp.concatenate([qf, jnp.zeros_like(qf)], axis=0).T.astype(BF16)
    do_nat = jnp.concatenate([jnp.zeros_like(dof), dof], axis=0).T.astype(BF16)
    spot = lax.broadcasted_iota(jnp.int32, (kb, qb), 0)
    level = lse[...]
    grad = jnp.zeros((HD, qb), F32)
    for r in range(groups):
        first = rows[r : r + 1, :]
        end = rows[groups + r : groups + r + 1, :]

        def step(j, grad, r=r, first=first, end=end):
            k0 = pl.multiple_of(j * kb, kb)
            at = pl.ds(r * count + k0, kb)
            kv = kvn[at, :]
            s = jnp.dot(kv, q_pad, preferred_element_type=F32)
            dp = jnp.dot(kv, do_pad, preferred_element_type=F32)
            p = jnp.where((spot >= first - k0) & (spot < end - k0), jnp.exp(s - level), 0.0)
            ds = (p * (dp - delta)).astype(BF16)
            acc[at, :] += jnp.dot(ds, q_nat, preferred_element_type=F32) + jnp.dot(
                p.astype(BF16), do_nat, preferred_element_type=F32
            )
            if r == 0:
                k = own[HD : 2 * HD, pl.ds(k0, kb)]
            else:
                k = oth[r - 1, 0:HD, pl.ds(k0, kb)]
            return grad + jnp.dot(k, ds, preferred_element_type=F32)

        grad = lax.fori_loop(
            lo[i * groups + r] // kb, (hi[i * groups + r] + kb - 1) // kb, step, grad
        )
    dq[...] = (grad * scale).astype(BF16)

    @pl.when(i == pl.num_programs(0) - 1)
    def _():
        chunk = min(count, 256)
        for r in range(groups):
            for c in range(count // chunk):
                at = slice(c * chunk, (c + 1) * chunk)
                piece = acc[r * count + c * chunk : r * count + (c + 1) * chunk, :].T
                if r == 0:
                    dkv[:, at] = piece
                else:
                    dkv_oth[r - 1, :, at] = piece.astype(BF16)


def blocks_of(count):
    return math.gcd(count, 256), math.gcd(count, 512)


def whole(shape):
    return pl.BlockSpec(shape, lambda i, *_: (0,) * len(shape))


def attention_forward(lo, hi, own, oth, rows, groups):
    count = own.shape[1]
    qb, kb = blocks_of(count)
    col = lambda height: pl.BlockSpec((height, qb), lambda i, *_: (0, i))
    return pl.pallas_call(
        functools.partial(forward_kernel, groups=groups, count=count, kb=kb),
        grid_spec=pltpu.PrefetchScalarGridSpec(
            num_scalar_prefetch=2,
            grid=(count // qb,),
            in_specs=[col(HD), whole(own.shape), whole(oth.shape), col(rows.shape[0])],
            out_specs=[col(HD), col(1)],
            scratch_shapes=[pltpu.VMEM((groups * count, 2 * HD), BF16)],
        ),
        out_shape=[
            jax.ShapeDtypeStruct((HD, count), BF16),
            jax.ShapeDtypeStruct((1, count), F32),
        ],
        name="attention_forward",
    )(lo, hi, own, own, oth, rows)


def attention_backward(lo, hi, own, oth, rows, out, do, lse, groups):
    count = own.shape[1]
    qb, kb = blocks_of(count)
    col = lambda height: pl.BlockSpec((height, qb), lambda i, *_: (0, i))
    others = (max(groups - 1, 1), 2 * HD, count)
    return pl.pallas_call(
        functools.partial(backward_kernel, groups=groups, count=count, kb=kb),
        grid_spec=pltpu.PrefetchScalarGridSpec(
            num_scalar_prefetch=2,
            grid=(count // qb,),
            in_specs=[
                col(HD), whole(own.shape), whole(oth.shape), col(rows.shape[0]),
                col(HD), col(HD), col(1),
            ],
            out_specs=[col(HD), whole((2 * HD, count)), whole(others)],
            scratch_shapes=[
                pltpu.VMEM((groups * count, 2 * HD), BF16),
                pltpu.VMEM((groups * count, 2 * HD), F32),
            ],
        ),
        out_shape=[
            jax.ShapeDtypeStruct((HD, count), BF16),
            jax.ShapeDtypeStruct((2 * HD, count), F32),
            jax.ShapeDtypeStruct(others, BF16),
        ],
        name="attention_backward",
    )(lo, hi, own, own, oth, rows, out, do, lse)


def layer(
    tokens,
    seq_ids,
    attention_norm_gain,
    qkv_weight,
    out_weight,
    feedforward_norm_gain,
    mlp_in_weight,
    mlp_out_weight,
    grad_out,
    *,
    ctx,
    tp,
):
    tok_rows, width = tokens.shape
    local_cols = qkv_weight.shape[2]
    heads_here = local_cols // HD
    hidden_here = mlp_in_weight.shape[2]
    groups = ctx // heads_here
    part = tok_rows // groups
    count = ctx * part
    me = lax.axis_index("ctx")

    def tp_sum(value):
        value = value.astype(BF16)
        if tp == 2:
            other = lax.ppermute(value, "tp", [(0, 1), (1, 0)])
            return value.astype(F32) + other.astype(F32)
        return lax.psum(value, "tp").astype(F32)

    def to_group(value, r):
        pairs = [(i, i // groups * groups + (i + r) % groups) for i in range(ctx)]
        return lax.ppermute(value, "ctx", pairs)

    def to_heads(value):
        rows = value.shape[1]
        value = value.reshape(heads_here, rows, groups, part).transpose(0, 2, 1, 3)
        value = lax.all_to_all(value.reshape(ctx, rows, part), "ctx", 0, 0)
        return value.transpose(1, 0, 2).reshape(rows, count)

    def to_tokens(value):
        rows = value.shape[0]
        value = value.reshape(rows, ctx, part).transpose(1, 0, 2)
        value = lax.all_to_all(value, "ctx", 0, 0)
        value = value.reshape(heads_here, groups, rows, part).transpose(0, 2, 1, 3)
        return value.reshape(heads_here, rows, tok_rows)

    def swap(value, bit):
        return lax.ppermute(value, "ctx", [(i, i ^ (1 << bit)) for i in range(ctx)])

    def ctx_sum(value, order):
        for bit in order:
            side = (me >> bit) & 1
            halves = value.reshape(2, value.shape[0] // 2, value.shape[1])
            send = lax.dynamic_index_in_dim(halves, 1 - side, 0, keepdims=False)
            keep = lax.dynamic_index_in_dim(halves, side, 0, keepdims=False)
            value = (keep.astype(F32) + swap(send, bit).astype(F32)).astype(BF16)
        for bit in reversed(order):
            side = (me >> bit) & 1
            other = swap(value, bit)
            value = jnp.concatenate(
                [jnp.where(side == 0, value, other), jnp.where(side == 0, other, value)], axis=0
            )
        return value

    bits = list(range(ctx.bit_length() - 1))
    order_a = bits
    order_b = bits[:1] + bits[2:3] + bits[1:2] + bits[3:]

    input_tokens = tokens.astype(F32)
    attention_standardized, attention_inverse_deviation, attention_normed_input = layer_normalize(
        input_tokens, attention_norm_gain
    )
    first = attention_normed_input.astype(BF16)
    qkv_flat = qkv_weight.reshape(width, 3 * local_cols)
    proj = lax.dot_general(
        qkv_flat, first, (((0,), (1,)), ((), ())), preferred_element_type=F32
    ).reshape(3, heads_here, HD, tok_rows)
    positions = me * tok_rows + jnp.arange(tok_rows, dtype=jnp.int32)
    cosine, sine = rope_tables_t(positions, HD)
    ids = jnp.broadcast_to(seq_ids.astype(BF16)[None, None, :], (heads_here, PAD, tok_rows))
    packed = jnp.concatenate(
        [
            rotate_t(proj[0], cosine, sine).astype(BF16),
            rotate_t(proj[1], cosine, sine).astype(BF16),
            proj[2].astype(BF16),
            ids,
        ],
        axis=1,
    )
    own = to_heads(packed)
    if groups > 1:
        oth = jnp.stack([to_group(own[HD:], groups - r) for r in range(1, groups)])
    else:
        oth = own[None, HD:]
    id_own = own[3 * HD]
    id_all = jnp.concatenate([id_own[None], oth[: groups - 1, 2 * HD]], axis=0)
    marks = jnp.arange(SEQS + 1, dtype=F32)
    below = jnp.sum((id_all.astype(F32)[:, None, :] < marks[None, :, None]).astype(jnp.int32), -1)
    first_key = jnp.zeros((groups, count), jnp.int32)
    end_key = jnp.zeros((groups, count), jnp.int32)
    for s in range(SEQS):
        hit = (id_own == s)[None, :]
        first_key = jnp.where(hit, below[:, s : s + 1], first_key)
        end_key = jnp.where(hit, below[:, s + 1 : s + 2], end_key)
    rows = jnp.concatenate([first_key, end_key], axis=0)
    qb, _ = blocks_of(count)
    lo = first_key[:, ::qb].T.reshape(-1)
    hi = end_key[:, qb - 1 :: qb].T.reshape(-1)
    att_head, lse = attention_forward(lo, hi, own, oth, rows, groups)
    attended = to_tokens(att_head).reshape(local_cols, tok_rows)
    attn_part = lax.dot_general(
        attended, out_weight, (((0,), (0,)), ((), ())), preferred_element_type=F32
    )
    residual_middle = input_tokens + tp_sum(attn_part)
    feedforward_standardized, feedforward_inverse_deviation, feedforward_normed_input = (
        layer_normalize(residual_middle, feedforward_norm_gain)
    )
    second = feedforward_normed_input.astype(BF16)
    in_act = mlp_in_weight[:, 0]
    in_gate = mlp_in_weight[:, 1]
    act_in = jnp.dot(second, in_act, preferred_element_type=F32)
    gate = jnp.dot(second, in_gate, preferred_element_type=F32)
    hidden = (gelu_value(act_in) * gate).astype(BF16)
    upstream = grad_out.astype(F32)
    grad_hidden = lax.dot_general(
        grad_out, mlp_out_weight, (((1,), (1,)), ((), ())), preferred_element_type=F32
    )
    grad_act = (grad_hidden * gate * gelu_slope(act_in)).astype(BF16)
    grad_gate = (grad_hidden * gelu_value(act_in)).astype(BF16)
    over_cols = (((1,), (1,)), ((), ()))
    over_rows = (((0,), (0,)), ((), ()))
    second_part = lax.dot_general(
        grad_act, in_act, over_cols, preferred_element_type=F32
    ) + lax.dot_general(grad_gate, in_gate, over_cols, preferred_element_type=F32)
    feedforward_norm_gradient = tp_sum(second_part)
    grad_w_act = lax.dot_general(second, grad_act, over_rows, preferred_element_type=F32)
    grad_w_gate = lax.dot_general(second, grad_gate, over_rows, preferred_element_type=F32)
    grad_w_out = lax.dot_general(hidden, grad_out, over_rows, preferred_element_type=F32)
    sum_act, sum_gate, sum_w_out = (
        lax.psum(value.astype(BF16), "ctx").astype(F32)
        for value in (grad_w_act, grad_w_gate, grad_w_out)
    )
    ffn_part = jnp.dot(hidden, mlp_out_weight, preferred_element_type=F32)
    output = (residual_middle + tp_sum(ffn_part)).astype(BF16)
    feedforward_normed_gradient, feedforward_gain_gradient = layer_normalize_backward(
        feedforward_norm_gradient,
        feedforward_standardized,
        feedforward_inverse_deviation,
        feedforward_norm_gain,
    )
    grad_mid = upstream + feedforward_normed_gradient
    grad_mid_b = grad_mid.astype(BF16)
    grad_att = (
        lax.dot_general(out_weight, grad_mid_b, over_cols, preferred_element_type=F32)
        .astype(BF16)
        .reshape(heads_here, HD, tok_rows)
    )
    do_head = to_heads(grad_att)
    dq, dkv, dkv_oth = attention_backward(
        lo, hi, own, oth, rows, att_head, do_head, lse, groups
    )
    for r in range(1, groups):
        dkv = dkv + to_group(dkv_oth[r - 1], r).astype(F32)
    grads = to_tokens(jnp.concatenate([dq, dkv.astype(BF16)], axis=0)).astype(F32)
    grad_proj = (
        jnp.stack(
            [
                unrotate_t(grads[:, :HD], cosine, sine),
                unrotate_t(grads[:, HD : 2 * HD], cosine, sine),
                grads[:, 2 * HD :],
            ]
        )
        .astype(BF16)
        .reshape(3 * local_cols, tok_rows)
    )
    first_part = lax.dot_general(
        grad_proj, qkv_flat, (((0,), (1,)), ((), ())), preferred_element_type=F32
    )
    attention_norm_gradient = tp_sum(first_part)
    grad_w_qkv = jnp.concatenate(
        [
            lax.dot_general(
                first,
                grad_proj[c * local_cols : (c + 1) * local_cols],
                (((0,), (1,)), ((), ())),
                preferred_element_type=F32,
            ).astype(BF16)
            for c in range(3)
        ],
        axis=0,
    )
    grad_w_attn = jnp.dot(attended, grad_mid_b, preferred_element_type=F32).astype(BF16)
    sum_attn = ctx_sum(grad_w_attn, order_a)
    middle = 3 * width // 2
    sum_qkv = (
        jnp.concatenate(
            [ctx_sum(grad_w_qkv[:middle], order_a), ctx_sum(grad_w_qkv[middle:], order_b)], axis=0
        )
        .reshape(3, width, local_cols)
        .transpose(1, 0, 2)
        .astype(F32)
    )
    attention_normed_gradient, attention_gain_gradient = layer_normalize_backward(
        attention_norm_gradient,
        attention_standardized,
        attention_inverse_deviation,
        attention_norm_gain,
    )
    grad_tokens = grad_mid + attention_normed_gradient
    gains = jnp.stack([attention_gain_gradient, feedforward_gain_gradient])
    for bit in bits:
        gains = gains + swap(gains, bit)
    return (
        output,
        grad_tokens,
        gains[0],
        sum_qkv,
        sum_attn.astype(F32),
        gains[1],
        jnp.stack([sum_act, sum_gate], axis=1),
        sum_w_out,
    )


def solution(mesh):
    return jax.shard_map(
        functools.partial(layer, ctx=mesh.shape["ctx"], tp=mesh.shape["tp"]),
        mesh=mesh,
        in_specs=(
            P("ctx", None),
            P("ctx"),
            P(),
            P(None, None, "tp"),
            P("tp", None),
            P(),
            P(None, None, "tp"),
            P("tp", None),
            P("ctx", None),
        ),
        out_specs=(
            P("ctx", None),
            P("ctx", None),
            P(),
            P(None, None, "tp"),
            P("tp", None),
            P(),
            P(None, None, "tp"),
            P("tp", None),
        ),
        check_vma=False,
    )
```

time: 706 us -> 450 us (0.64); the launches traced: 697 us -> 454 us
  waiting for transfers between devices: 405 us -> 198 us
  matrix products: 135 us -> 25.1 us
  Pallas kernels: 0 us -> 54.4 us
  starting transfers between devices: 0.71 us -> 44 us
  other arithmetic: 66.6 us -> 42.8 us
  blocking collectives: 58.2 us -> 41.9 us
  local copies, waits for them, and re-layouts: 16.6 us -> 32.6 us
    psum x4 -> x1, waiting for transfers between devices: 275 us -> 78.1 us  [layer(): lax.psum(value.astype(BF16), 'ctx').astype(F32)]
    ppermute x0 -> x34, waiting for transfers between devices: none -> 115 us  [the longest x28 73.1 us: swap(): return lax.ppermute(value, 'ctx', [(i, i ^ 1 << bit) for i in range(ctx)])]
    dot_general x18 -> x17, matrix products: 135 us -> 25.1 us  [the longest x1 3.67 us: layer(): lax.dot_general(second, grad_act, over_rows, preferred_element_type=F32)]
    reduce_scatter x1 -> x0, waiting for transfers between devices: 81.5 us -> none  [per_device(): lax.psum_scatter(pair.astype(jnp.bfloat16), 'ctx', scatter_dimension=0, t...]
    pallas_call x0 -> x2, Pallas kernels: none -> 54.4 us  [the longest x1 28.7 us: attention_backward(): pl.pallas_call(functools.partial(backward_kernel, groups=groups, count=co...]
    all_gather x2 -> x0, waiting for transfers between devices: 48.4 us -> none  [the longest x1 28.3 us: per_device(): key_piece = lax.all_gather(keys_flat, 'ctx', axis=0, tiled=True)]
    all_to_all x0 -> x2, blocking collectives: none -> 41.9 us  [the longest x1 28.5 us: to_heads(): value = lax.all_to_all(value.reshape(ctx, rows, part), 'ctx', 0, 0)]
    ppermute x0 -> x34, starting transfers between devices: none -> 36.1 us  [the longest x28 29.8 us: swap(): return lax.ppermute(value, 'ctx', [(i, i ^ 1 << bit) for i in range(ctx)])]
  transfers between devices with their start and end apart: 7 -> 37, of which waited for: 7 -> 24; matrix products, arithmetic and copies ran while one was open for 11% -> 11% of each run, Pallas kernels for 0% -> 6%
where the time goes in v1:
time: 450 us; the launch traced here: 454 us
  waiting for transfers between devices  198 us (44%)
  Pallas kernels  54.4 us (12%)
  starting transfers between devices  44 us (10%)
  other arithmetic  42.8 us (10%)
  blocking collectives  41.9 us (9%)
  local copies, waits for them, and re-layouts  32.6 us (7%)
  matrix products  25.1 us (6%)
  between operations  15.1 us (3%)
    psum x1, waiting for transfers between devices, layer(): lax.psum(value.astype(BF16), 'ctx').astype(F32)  78.1 us
    ppermute x28, waiting for transfers between devices, swap(): return lax.ppermute(value, 'ctx', [(i, i ^ 1 << bit) for i in range(ctx)])  73.1 us
    ppermute x4, waiting for transfers between devices, tp_sum(): other = lax.ppermute(value, 'tp', [(0, 1), (1, 0)])  41 us
    ppermute x28, starting transfers between devices, swap(): return lax.ppermute(value, 'ctx', [(i, i ^ 1 << bit) for i in range(ctx)])  29.8 us
    pallas_call x1, Pallas kernels, attention_backward(): pl.pallas_call(functools.partial(backward_kernel, groups=groups, count=co...  28.7 us
    all_to_all x1, blocking collectives, to_heads(): value = lax.all_to_all(value.reshape(ctx, rows, part), 'ctx', 0, 0)  28.5 us
    pallas_call x1, Pallas kernels, attention_forward(): pl.pallas_call(functools.partial(forward_kernel, groups=groups, count=cou...  25.7 us
    unnamed x86, local copies, waits for them, and re-layouts  14 us
  transfers between devices with their start and end apart: 37, of which 24 were waited for; matrix products, arithmetic and copies ran while one was open for 11% of the time, Pallas kernels for 6%

profile of v1, /device:TPU:0, one launch (start us, length us, event | category | flops | bytes accessed | tf_op | source)
XLA Modules:
  0.0 453.6 jit_solution(6748806545247709095)
XLA Ops:
  9.9 4.7 %copy.60 = bf16[1024,3,512]{0,2,1:T(8,128)(2,1)} copy(bf16[1024,3,512]{2,0,1:T(8,128)(2,1)} %param.12) | data formatting | bytes 6291456 | tf_op args[3]
  14.6 3.0 convolution_bitcast_fusion
  19.2 2.0 copy.62
  22.1 2.1 copy.61
  28.0 28.5 %all_to_all.20 = bf16[16,208,128]{2,1,0:T(8,128)(2,1)S(1)} all-to-all(bf16[16,208,128]{2,1,0:T(8,128)(2,1)S(1)} %bitcast.224), channel_id=1, replica_groups=mesh['ctx'=16,'tp'=2] {'ctx'}, dimensions={0} | all-to-all | bytes 1703936 | tf_op jit(solution)/shard_map/all_to_all | solution.py:292
  62.7 25.7 %attention_forward.1 = (bf16[64,2048]{1,0:T(8,128)(2,1)}, f32[1,2048]{1,0:T(1,128)}) custom-call(s32[16]{0:T(128)} %reshape.297.lo, s32[16]{0:T(128)} %reshape.298.hi, bf16[208,2048]{1,0:T(8,128)(2,1)} %copy_bitcast_fusion.q_ref.own, bf16[208,2048]{1,0:T(8,128)(2,1)} %copy_bitcast_fusion.q_ref.own, bf16[1,144,2048]{2,1,0:T(8,128)(2,1)} %bitcast.234, ...), custom_call_target="tpu_custom_call" | custom-call | tf_op jit(solution)/shard_map/attention_forward/pallas_call | solution.py:209
  89.4 13.4 %all_to_all.21 = bf16[16,64,128]{2,1,0:T(8,128)(2,1)S(1)} all-to-all(bf16[16,64,128]{2,1,0:T(8,128)(2,1)S(1)} %bitcast_bitcast_fusion.1), channel_id=1, replica_groups=mesh['ctx'=16,'tp'=2] {'ctx'}, dimensions={0} | all-to-all | bytes 524288 | tf_op jit(solution)/shard_map/all_to_all | solution.py:298
  103.2 1.8 convolution_convert_fusion.7
  107.5 11.3 %collective-permute-done.1 = bf16[256,1024]{1,0:T(8,128)(2,1)S(1)} collective-permute-done((bf16[256,1024]{1,0:T(8,128)(2,1)S(1)}, bf16[256,1024]{1,0:T(8,128)(2,1)S(1)}, u32[]{:S(2)}, u32[]{:S(2)}) %collective-permute-start.1) | collective-permute-done | bytes 524320 | tf_op jit(solution)/shard_map/ppermute | solution.py:281
  130.0 11.3 %collective-permute-done.3 = bf16[256,1024]{1,0:T(8,128)(2,1)} collective-permute-done((bf16[256,1024]{1,0:T(8,128)(2,1)}, bf16[256,1024]{1,0:T(8,128)(2,1)}, u32[]{:S(2)}, u32[]{:S(2)}) %collective-permute-start.3) | collective-permute-done | bytes 524320 | tf_op jit(solution)/shard_map/ppermute | solution.py:281
  141.2 2.1 multiply_reduce_fusion
  143.3 7.2 %collective-permute-done.2 = bf16[256,1024]{1,0:T(8,128)(2,1)S(1)} collective-permute-done((bf16[256,1024]{1,0:T(8,128)(2,1)}, bf16[256,1024]{1,0:T(8,128)(2,1)S(1)}, u32[]{:S(2)}, u32[]{:S(2)}) %collective-permute-start.2) | collective-permute-done | bytes 524320 | tf_op jit(solution)/shard_map/ppermute | solution.py:281
  151.3 2.8 multiply_add_fusion
  156.3 2.2 collective-permute-done.26
  163.6 4.0 all-to-all-start.2
  167.7 2.5 collective-permute-done.27
  172.6 5.2 %collective-permute-done.28 = bf16[64,1024]{1,0:T(8,128)(2,1)S(1)} collective-permute-done((bf16[64,1024]{1,0:T(8,128)(2,1)S(1)}, bf16[64,1024]{1,0:T(8,128)(2,1)S(1)}, u32[]{:S(2)}, u32[]{:S(2)}) %collective-permute-start.28) | collective-permute-done | bytes 131104 | tf_op jit(solution)/shard_map/ppermute | solution.py:303
  177.8 2.4 collective-permute-start.29
  181.0 28.7 %attention_backward.1 = (bf16[64,2048]{1,0:T(8,128)(2,1)}, f32[128,2048]{1,0:T(8,128)}, bf16[1,128,2048]{2,1,0:T(8,128)(2,1)}) custom-call(s32[16]{0:T(128)} %reshape.297.lo, s32[16]{0:T(128)} %reshape.298.hi, bf16[208,2048]{1,0:T(8,128)(2,1)} %copy_bitcast_fusion.q_ref.own, bf16[208,2048]{1,0:T(8,128)(2,1)} %copy_bitcast_fusion.q_ref.own, ...), custom_call_target="tpu_custom_call" | custom-call | tf_op jit(solution)/shard_map/attention_backward/pallas_call | solution.py:231
  210.5 6.2 %collective-permute-done.30 = bf16[32,1024]{1,0:T(8,128)(2,1)S(1)} collective-permute-done((bf16[32,1024]{1,0:T(8,128)(2,1)S(1)}, bf16[32,1024]{1,0:T(8,128)(2,1)S(1)}, u32[]{:S(2)}, u32[]{:S(2)}) %collective-permute-start.30) | collective-permute-done | bytes 65568 | tf_op jit(solution)/shard_map/ppermute | solution.py:303
  219.1 3.1 collective-permute-done.31
  224.9 3.8 all-to-all-start.3
  228.9 3.7 fusion
  234.8 2.4 fusion.1
  237.2 2.4 convolution_convert_fusion.2
  242.4 5.0 %all-to-all-done.3 = bf16[16,192,128]{2,1,0:T(8,128)(2,1)S(1)} async-done(((bf16[16,192,128]{2,1,0:T(8,128)(2,1)}), bf16[16,192,128]{2,1,0:T(8,128)(2,1)S(1)}, u32[]{:S(2)}, u32[]{:S(2)}) %all-to-all-start.3) | async-done | bytes 786464 | tf_op jit(solution)/shard_map/all_to_all | solution.py:298
  249.1 2.5 convert_element_type.335
  260.4 11.2 %collective-permute-done.5 = bf16[256,1024]{1,0:T(8,128)(2,1)S(1)} collective-permute-done((bf16[256,1024]{1,0:T(8,128)(2,1)S(1)}, bf16[256,1024]{1,0:T(8,128)(2,1)S(1)}, u32[]{:S(2)}, u32[]{:S(2)}) %collective-permute-start.5) | collective-permute-done | bytes 524320 | tf_op jit(solution)/shard_map/ppermute | solution.py:281
  275.0 2.2 collective-permute-done.7
  277.2 2.7 collective-permute-start.8
  279.9 1.9 collective-permute-done.8
  281.8 2.0 collective-permute-start.9
  285.4 2.1 collective-permute-start.19
  288.9 4.6 %collective-permute-done.11 = bf16[384,512]{1,0:T(8,128)(2,1)S(1)} collective-permute-done((bf16[384,512]{1,0:T(8,128)(2,1)S(1)}, bf16[384,512]{1,0:T(8,128)(2,1)S(1)}, u32[]{:S(2)}, u32[]{:S(2)}) %collective-permute-start.11) | collective-permute-done | bytes 393248 | tf_op jit(solution)/shard_map/ppermute | solution.py:303
  295.0 10.8 %collective-permute-done.19 = bf16[384,512]{1,0:T(8,128)(2,1)S(1)} collective-permute-done((bf16[384,512]{1,0:T(8,128)(2,1)S(1)}, bf16[384,512]{1,0:T(8,128)(2,1)S(1)}, u32[]{:S(2)}, u32[]{:S(2)}) %collective-permute-start.19) | collective-permute-done | bytes 393248 | tf_op jit(solution)/shard_map/ppermute | solution.py:303
  307.1 4.6 %collective-permute-done.12 = bf16[192,512]{1,0:T(8,128)(2,1)S(1)} collective-permute-done((bf16[192,512]{1,0:T(8,128)(2,1)S(1)}, bf16[192,512]{1,0:T(8,128)(2,1)S(1)}, u32[]{:S(2)}, u32[]{:S(2)}) %collective-permute-start.12) | collective-permute-done | bytes 196640 | tf_op jit(solution)/shard_map/ppermute | solution.py:303
  311.8 2.5 collective-permute-start.13
  315.0 6.5 %collective-permute-done.13 = bf16[96,512]{1,0:T(8,128)(2,1)S(1)} collective-permute-done((bf16[96,512]{1,0:T(8,128)(2,1)S(1)}, bf16[96,512]{1,0:T(8,128)(2,1)S(1)}, u32[]{:S(2)}, u32[]{:S(2)}) %collective-permute-start.13) | collective-permute-done | bytes 98336 | tf_op jit(solution)/shard_map/ppermute | solution.py:303
  321.6 7.3 %collective-permute-done.21 = bf16[96,512]{1,0:T(8,128)(2,1)S(1)} collective-permute-done((bf16[96,512]{1,0:T(8,128)(2,1)S(1)}, bf16[96,512]{1,0:T(8,128)(2,1)S(1)}, u32[]{:S(2)}, u32[]{:S(2)}) %collective-permute-start.21) | collective-permute-done | bytes 98336 | tf_op jit(solution)/shard_map/ppermute | solution.py:303
  329.0 8.4 %collective-permute-done.14 = bf16[96,512]{1,0:T(8,128)(2,1)S(1)} collective-permute-done((bf16[96,512]{1,0:T(8,128)(2,1)S(1)}, bf16[96,512]{1,0:T(8,128)(2,1)S(1)}, u32[]{:S(2)}, u32[]{:S(2)}) %collective-permute-start.14) | collective-permute-done | bytes 98336 | tf_op jit(solution)/shard_map/ppermute | solution.py:303
  337.5 3.2 collective-permute-start.15
  340.7 1.9 collective-permute-done.22
  345.2 2.0 collective-permute-start.16
  347.2 3.7 collective-permute-done.23
  351.7 78.1 %all-reduce.3.cloned.1.call-done = (bf16[1024,1,1312]{0,2,1:T(8,128)(2,1)}, bf16[1024,1,1312]{0,2,1:T(8,128)(2,1)}, bf16[1312,1024]{1,0:T(8,128)(2,1)}) async-done(((bf16[1024,1,1312]{0,2,1:T(8,128)(2,1)}, bf16[1024,1,1312]{0,2,1:T(8,128)(2,1)}, bf16[1312,1024]{1,0:T(8,128)(2,1)}), (bf16[1024,1,1312]{0,2,1:T(8,128)(2,1)}, bf16[1024,1,1312]{0,2,1:T(8,128)(2,1)}, ...) | async-done | bytes 8060944 | tf_op jit(solution)/shard_map/psum | solution.py:395
  429.9 4.8 %convert_element_type.400 = f32[1312,1024]{1,0:T(8,128)} convert(bf16[1312,1024]{1,0:T(8,128)(2,1)} %get-tuple-element.30) | non-fusion elementwise | flops 1343488 | bytes 8060928 | tf_op jit(solution)/shard_map/convert_element_type | solution.py:395
  437.3 4.9 %maximum_convert_fusion = f32[1024,2,1312]{0,2,1:T(8,128)} fusion(bf16[1024,1,1312]{0,2,1:T(8,128)(2,1)S(1)} %copy-done.12, bf16[1024,1,1312]{0,2,1:T(8,128)(2,1)S(1)} %copy-done.13), kind=kLoop, calls=%fused_computation.1 | loop fusion | flops 5373952 | bytes 16121856 | tf_op jit(solution)/shard_map/stack | solution.py:475
  443.1 3.6 convert_bitcast_fusion
  (256 shorter events, 79.4 us)
Async XLA Ops:
  7.2 99.4 %copy-start = (bf16[1312,1024]{1,0:T(8,128)(2,1)S(1)}, bf16[1312,1024]{1,0:T(8,128)(2,1)}, u32[]{:S(2)}) copy-start(bf16[1312,1024]{1,0:T(8,128)(2,1)} %param.16) | copy-start | bytes 8060932
  56.6 2.7 collective-permute-start
  88.4 18.2 %copy-start.5 = (bf16[256,1024]{1,0:T(8,128)(2,1)S(1)}, bf16[256,1024]{1,0:T(8,128)(2,1)}, u32[]{:S(2)}) copy-start(bf16[256,1024]{1,0:T(8,128)(2,1)} %param.17) | copy-start | bytes 1572868
  103.1 17.5 %slice-start = ((s8[5373952]{0:T(1024)(128)(4,1)}), s8[4194304]{0:T(1024)(128)(4,1)S(1)}, s32[]{:S(2)}) async-start(s8[5373952]{0:T(1024)(128)(4,1)} %bitcast.244), calls=%async_computation.5 | async-start | bytes 8388608
  105.0 15.6 %slice-start.1 = ((s8[5373952]{0:T(1024)(128)(4,1)}), s8[1179648]{0:T(1024)(128)(4,1)S(1)}, s32[]{:S(2)}) async-start(s8[5373952]{0:T(1024)(128)(4,1)} %bitcast.244), calls=%async_computation.6 | async-start | bytes 2359296
  105.0 13.8 %collective-permute-start.1 = (bf16[256,1024]{1,0:T(8,128)(2,1)S(1)}, bf16[256,1024]{1,0:T(8,128)(2,1)S(1)}, u32[]{:S(2)}, u32[]{:S(2)}) collective-permute-start(bf16[256,1024]{1,0:T(8,128)(2,1)S(1)} %convolution_convert_fusion.7), channel_id=1, source_target_pairs={{0,1},{1,0},{2,3},{3,2},{4,5},{5,4},{6,7},{7,6},{8,9},{9,8},{10,11... | collective-permute-start | bytes 1572872 | tf_op jit(solution)/shard_map/ppermute | solution.py:281
  107.5 12.6 %copy-start.30 = (f32[1024]{0:T(1024)S(1)}, f32[1024]{0:T(1024)}, u32[]{:S(2)}) copy-start(f32[1024]{0:T(1024)} %param.14) | copy-start | bytes 12292
  126.1 15.1 %collective-permute-start.3 = (bf16[256,1024]{1,0:T(8,128)(2,1)}, bf16[256,1024]{1,0:T(8,128)(2,1)}, u32[]{:S(2)}, u32[]{:S(2)}) collective-permute-start(bf16[256,1024]{1,0:T(8,128)(2,1)} %fusion.25), channel_id=1, source_target_pairs={{0,1},{1,0},{2,3},{3,2},{4,5},{5,4},{6,7},{7,6},{8,9},{9,8},{10,11... | collective-permute-start | bytes 1572872 | tf_op jit(solution)/shard_map/ppermute | solution.py:281
  129.4 21.8 %copy-start.3 = (f32[256,1024]{1,0:T(8,128)S(1)}, f32[256,1024]{1,0:T(8,128)}, u32[]{:S(2)}) copy-start(f32[256,1024]{1,0:T(8,128)} %copy-done.2) | copy-start | bytes 3145732
  129.4 21.8 %copy-start.6 = (bf16[256,1024]{1,0:T(8,128)(2,1)S(1)}, bf16[256,1024]{1,0:T(8,128)(2,1)}, u32[]{:S(2)}) copy-start(bf16[256,1024]{1,0:T(8,128)(2,1)} %param.17) | copy-start | bytes 1572868
  129.4 21.8 %copy-start.33 = (f32[256]{0:T(256)S(1)}, f32[256]{0:T(256)}, u32[]{:S(2)}) copy-start(f32[256]{0:T(256)} %copy-done.32) | copy-start | bytes 3076
  129.4 21.0 %collective-permute-start.2 = (bf16[256,1024]{1,0:T(8,128)(2,1)}, bf16[256,1024]{1,0:T(8,128)(2,1)S(1)}, u32[]{:S(2)}, u32[]{:S(2)}) collective-permute-start(bf16[256,1024]{1,0:T(8,128)(2,1)} %convolution_convert_fusion.8), channel_id=1, source_target_pairs={{0,1},{1,0},{2,3},{3,2},{4,5},{5,4},{6,7},{7,6},{8,9},{9,8},{10,11... | collective-permute-start | bytes 1572872 | tf_op jit(solution)/shard_map/ppermute | solution.py:281
  154.5 7.7 %copy-start.9 = (bf16[512,1024]{1,0:T(8,128)(2,1)S(1)}, bf16[512,1024]{1,0:T(8,128)(2,1)}, u32[]{:S(2)}) copy-start(bf16[512,1024]{1,0:T(8,128)(2,1)} %param.13) | copy-start | bytes 3145732
  156.3 2.3 collective-permute-start.26
  161.5 8.7 %collective-permute-start.27 = (bf16[128,1024]{1,0:T(8,128)(2,1)}, bf16[128,1024]{1,0:T(8,128)(2,1)}, u32[]{:S(2)}, u32[]{:S(2)}) collective-permute-start(bf16[128,1024]{1,0:T(8,128)(2,1)} %dynamic-slice_bitcast_fusion.5), channel_id=1, source_target_pairs={{0,4},{2,6},{4,0},{6,2},{8,12},{10,14},{12,8},{14,10},{16,20},{18,... | collective-permute-start | bytes 786440 | tf_op jit(solution)/shard_map/ppermute | solution.py:303
  162.7 7.5 %copy-start.18 = (bf16[256,1024]{1,0:T(8,128)(2,1)S(1)}, bf16[256,1024]{1,0:T(8,128)(2,1)}, u32[]{:S(2)}) copy-start(bf16[256,1024]{1,0:T(8,128)(2,1)} %copy-done.17) | copy-start | bytes 1572868
  163.6 16.6 %all-to-all-start.2 = ((bf16[16,64,128]{2,1,0:T(8,128)(2,1)}), bf16[16,64,128]{2,1,0:T(8,128)(2,1)S(1)}, u32[]{:S(2)}, u32[]{:S(2)}) async-start(bf16[16,64,128]{2,1,0:T(8,128)(2,1)} %bitcast.24), calls=%async_computation.2 | async-start | bytes 524288 | tf_op jit(solution)/shard_map/all_to_all | solution.py:292
  171.2 6.6 %collective-permute-start.28 = (bf16[64,1024]{1,0:T(8,128)(2,1)S(1)}, bf16[64,1024]{1,0:T(8,128)(2,1)S(1)}, u32[]{:S(2)}, u32[]{:S(2)}) collective-permute-start(bf16[64,1024]{1,0:T(8,128)(2,1)S(1)} %dynamic-slice_bitcast_fusion.8), channel_id=1, source_target_pairs={{0,8},{2,10},{4,12},{6,14},{8,0},{10,2},{12,4},{14,6},{16,24},{18,... | collective-permute-start | bytes 393224 | tf_op jit(solution)/shard_map/ppermute | solution.py:303
  177.8 32.0 %collective-permute-start.29 = (bf16[32,1024]{1,0:T(8,128)(2,1)S(1)}, bf16[32,1024]{1,0:T(8,128)(2,1)S(1)}, u32[]{:S(2)}, u32[]{:S(2)}) collective-permute-start(bf16[32,1024]{1,0:T(8,128)(2,1)S(1)} %dynamic-slice_bitcast_fusion.11), channel_id=1, source_target_pairs={{0,16},{2,18},{4,20},{6,22},{8,24},{10,26},{12,28},{14,30},{16,0},... | collective-permute-start | bytes 196616 | tf_op jit(solution)/shard_map/ppermute | solution.py:303
  209.7 7.1 %collective-permute-start.4 = (bf16[128,2048]{1,0:T(8,128)(2,1)}, bf16[128,2048]{1,0:T(8,128)(2,1)S(1)}, u32[]{:S(2)}, u32[]{:S(2)}) collective-permute-start(bf16[128,2048]{1,0:T(8,128)(2,1)} %bitcast.275), channel_id=1, source_target_pairs={{0,2},{2,0},{4,6},{6,4},{8,10},{10,8},{12,14},{14,12},{16,18},{18,... | collective-permute-start | bytes 1572872 | tf_op jit(solution)/shard_map/ppermute | solution.py:287
  209.9 6.8 %collective-permute-start.30 = (bf16[32,1024]{1,0:T(8,128)(2,1)S(1)}, bf16[32,1024]{1,0:T(8,128)(2,1)S(1)}, u32[]{:S(2)}, u32[]{:S(2)}) collective-permute-start(bf16[32,1024]{1,0:T(8,128)(2,1)S(1)} %fusion.66), channel_id=1, source_target_pairs={{0,16},{2,18},{4,20},{6,22},{8,24},{10,26},{12,28},{14,30},{16,0},... | collective-permute-start | bytes 196616 | tf_op jit(solution)/shard_map/ppermute | solution.py:303
  210.5 13.4 %copy-start.29 = (bf16[64,2048]{1,0:T(8,128)(2,1)S(1)}, bf16[64,2048]{1,0:T(8,128)(2,1)}, u32[]{:S(2)}) copy-start(bf16[64,2048]{1,0:T(8,128)(2,1)} %get-tuple-element.15) | copy-start | bytes 786436
  216.7 5.5 %collective-permute-start.31 = (bf16[64,1024]{1,0:T(8,128)(2,1)S(1)}, bf16[64,1024]{1,0:T(8,128)(2,1)S(1)}, u32[]{:S(2)}, u32[]{:S(2)}) collective-permute-start(bf16[64,1024]{1,0:T(8,128)(2,1)S(1)} %pad_maximum_fusion.15), channel_id=1, source_target_pairs={{0,8},{2,10},{4,12},{6,14},{8,0},{10,2},{12,4},{14,6},{16,24},{18,... | collective-permute-start | bytes 393224 | tf_op jit(solution)/shard_map/ppermute | solution.py:303
  222.3 10.2 %collective-permute-start.32 = (bf16[128,1024]{1,0:T(8,128)(2,1)S(1)}, bf16[128,1024]{1,0:T(8,128)(2,1)}, u32[]{:S(2)}, u32[]{:S(2)}) collective-permute-start(bf16[128,1024]{1,0:T(8,128)(2,1)S(1)} %pad_maximum_fusion.12), channel_id=1, source_target_pairs={{0,4},{2,6},{4,0},{6,2},{8,12},{10,14},{12,8},{14,10},{16,20},{18,... | collective-permute-start | bytes 786440 | tf_op jit(solution)/shard_map/ppermute | solution.py:303
  224.9 22.5 %all-to-all-start.3 = ((bf16[16,192,128]{2,1,0:T(8,128)(2,1)}), bf16[16,192,128]{2,1,0:T(8,128)(2,1)S(1)}, u32[]{:S(2)}, u32[]{:S(2)}) async-start(bf16[16,192,128]{2,1,0:T(8,128)(2,1)} %bitcast_bitcast_fusion), calls=%async_computation.3 | async-start | bytes 1572864 | tf_op jit(solution)/shard_map/all_to_all | solution.py:298
  228.8 201.1 %all-reduce.3.cloned.1.call-start = ((), (), s32[]{:S(2)}) async-start(), calls=%async_computation.4 | async-start | bytes 16121856 | tf_op jit(solution)/shard_map/psum | solution.py:395
  234.6 5.1 %collective-permute-start.33 = (bf16[256,1024]{1,0:T(8,128)(2,1)}, bf16[256,1024]{1,0:T(8,128)(2,1)}, u32[]{:S(2)}, u32[]{:S(2)}) collective-permute-start(bf16[256,1024]{1,0:T(8,128)(2,1)} %pad_maximum_fusion.7), channel_id=1, source_target_pairs={{0,2},{2,0},{4,6},{6,4},{8,10},{10,8},{12,14},{14,12},{16,18},{18,... | collective-permute-start | bytes 1572872 | tf_op jit(solution)/shard_map/ppermute | solution.py:303
  257.4 14.3 %collective-permute-start.5 = (bf16[256,1024]{1,0:T(8,128)(2,1)S(1)}, bf16[256,1024]{1,0:T(8,128)(2,1)S(1)}, u32[]{:S(2)}, u32[]{:S(2)}) collective-permute-start(bf16[256,1024]{1,0:T(8,128)(2,1)S(1)} %convolution_convert_fusion.9), channel_id=1, source_target_pairs={{0,1},{1,0},{2,3},{3,2},{4,5},{5,4},{6,7},{7,6},{8,9},{9,8},{10,11... | collective-permute-start | bytes 1572872 | tf_op jit(solution)/shard_map/ppermute | solution.py:281
  272.2 1.2 collective-permute-start.6
  272.4 11.5 %collective-permute-start.10 = (bf16[768,512]{1,0:T(8,128)(2,1)S(1)}, bf16[768,512]{1,0:T(8,128)(2,1)S(1)}, u32[]{:S(2)}, u32[]{:S(2)}) collective-permute-start(bf16[768,512]{1,0:T(8,128)(2,1)S(1)} %dynamic-slice_bitcast_fusion.1), channel_id=1, source_target_pairs={{0,2},{2,0},{4,6},{6,4},{8,10},{10,8},{12,14},{14,12},{16,18},{18,... | collective-permute-start | bytes 2359304 | tf_op jit(solution)/shard_map/ppermute | solution.py:303
  272.9 12.2 %collective-permute-start.18 = (bf16[768,512]{1,0:T(8,128)(2,1)S(1)}, bf16[768,512]{1,0:T(8,128)(2,1)S(1)}, u32[]{:S(2)}, u32[]{:S(2)}) collective-permute-start(bf16[768,512]{1,0:T(8,128)(2,1)S(1)} %dynamic-slice_bitcast_fusion), channel_id=1, source_target_pairs={{0,2},{2,0},{4,6},{6,4},{8,10},{10,8},{12,14},{14,12},{16,18},{18,... | collective-permute-start | bytes 2359304 | tf_op jit(solution)/shard_map/ppermute | solution.py:303
  273.5 3.7 collective-permute-start.7
  277.2 4.6 %collective-permute-start.8 = (f32[2,1024]{1,0:T(2,128)S(1)}, f32[2,1024]{1,0:T(2,128)S(1)}, u32[]{:S(2)}, u32[]{:S(2)}) collective-permute-start(f32[2,1024]{1,0:T(2,128)S(1)} %fusion.103), channel_id=1, source_target_pairs={{0,8},{2,10},{4,12},{6,14},{8,0},{10,2},{12,4},{14,6},{16,24},{18,... | collective-permute-start | bytes 24584 | tf_op jit(solution)/shard_map/ppermute | solution.py:303
  281.8 7.1 %collective-permute-start.9 = (f32[2,1024]{1,0:T(2,128)S(1)}, f32[2,1024]{1,0:T(2,128)S(1)}, u32[]{:S(2)}, u32[]{:S(2)}) collective-permute-start(f32[2,1024]{1,0:T(2,128)S(1)} %add.224), channel_id=1, source_target_pairs={{0,16},{2,18},{4,20},{6,22},{8,24},{10,26},{12,28},{14,30},{16,0},... | collective-permute-start | bytes 24584 | tf_op jit(solution)/shard_map/ppermute | solution.py:303
  284.1 9.5 %collective-permute-start.11 = (bf16[384,512]{1,0:T(8,128)(2,1)S(1)}, bf16[384,512]{1,0:T(8,128)(2,1)S(1)}, u32[]{:S(2)}, u32[]{:S(2)}) collective-permute-start(bf16[384,512]{1,0:T(8,128)(2,1)S(1)} %dynamic-slice_bitcast_fusion.4), channel_id=1, source_target_pairs={{0,4},{2,6},{4,0},{6,2},{8,12},{10,14},{12,8},{14,10},{16,20},{18,... | collective-permute-start | bytes 1179656 | tf_op jit(solution)/shard_map/ppermute | solution.py:303
  285.4 20.5 %collective-permute-start.19 = (bf16[384,512]{1,0:T(8,128)(2,1)S(1)}, bf16[384,512]{1,0:T(8,128)(2,1)S(1)}, u32[]{:S(2)}, u32[]{:S(2)}) collective-permute-start(bf16[384,512]{1,0:T(8,128)(2,1)S(1)} %dynamic-slice_bitcast_fusion.3), channel_id=1, source_target_pairs={{0,8},{2,10},{4,12},{6,14},{8,0},{10,2},{12,4},{14,6},{16,24},{18,... | collective-permute-start | bytes 1179656 | tf_op jit(solution)/shard_map/ppermute | solution.py:303
  293.7 18.0 %collective-permute-start.12 = (bf16[192,512]{1,0:T(8,128)(2,1)S(1)}, bf16[192,512]{1,0:T(8,128)(2,1)S(1)}, u32[]{:S(2)}, u32[]{:S(2)}) collective-permute-start(bf16[192,512]{1,0:T(8,128)(2,1)S(1)} %dynamic-slice_bitcast_fusion.7), channel_id=1, source_target_pairs={{0,8},{2,10},{4,12},{6,14},{8,0},{10,2},{12,4},{14,6},{16,24},{18,... | collective-permute-start | bytes 589832 | tf_op jit(solution)/shard_map/ppermute | solution.py:303
  306.0 8.3 %collective-permute-start.20 = (bf16[192,512]{1,0:T(8,128)(2,1)S(1)}, bf16[192,512]{1,0:T(8,128)(2,1)S(1)}, u32[]{:S(2)}, u32[]{:S(2)}) collective-permute-start(bf16[192,512]{1,0:T(8,128)(2,1)S(1)} %dynamic-slice_bitcast_fusion.6), channel_id=1, source_target_pairs={{0,4},{2,6},{4,0},{6,2},{8,12},{10,14},{12,8},{14,10},{16,20},{18,... | collective-permute-start | bytes 589832 | tf_op jit(solution)/shard_map/ppermute | solution.py:303
  311.8 9.7 %collective-permute-start.13 = (bf16[96,512]{1,0:T(8,128)(2,1)S(1)}, bf16[96,512]{1,0:T(8,128)(2,1)S(1)}, u32[]{:S(2)}, u32[]{:S(2)}) collective-permute-start(bf16[96,512]{1,0:T(8,128)(2,1)S(1)} %dynamic-slice_bitcast_fusion.10), channel_id=1, source_target_pairs={{0,16},{2,18},{4,20},{6,22},{8,24},{10,26},{12,28},{14,30},{16,0},... | collective-permute-start | bytes 294920 | tf_op jit(solution)/shard_map/ppermute | solution.py:303
  314.4 14.6 %collective-permute-start.21 = (bf16[96,512]{1,0:T(8,128)(2,1)S(1)}, bf16[96,512]{1,0:T(8,128)(2,1)S(1)}, u32[]{:S(2)}, u32[]{:S(2)}) collective-permute-start(bf16[96,512]{1,0:T(8,128)(2,1)S(1)} %dynamic-slice_bitcast_fusion.9), channel_id=1, source_target_pairs={{0,16},{2,18},{4,20},{6,22},{8,24},{10,26},{12,28},{14,30},{16,0},... | collective-permute-start | bytes 294920 | tf_op jit(solution)/shard_map/ppermute | solution.py:303
  321.5 15.9 %collective-permute-start.14 = (bf16[96,512]{1,0:T(8,128)(2,1)S(1)}, bf16[96,512]{1,0:T(8,128)(2,1)S(1)}, u32[]{:S(2)}, u32[]{:S(2)}) collective-permute-start(bf16[96,512]{1,0:T(8,128)(2,1)S(1)} %fusion.61), channel_id=1, source_target_pairs={{0,16},{2,18},{4,20},{6,22},{8,24},{10,26},{12,28},{14,30},{16,0},... | collective-permute-start | bytes 294920 | tf_op jit(solution)/shard_map/ppermute | solution.py:303
  329.0 13.7 %collective-permute-start.22 = (bf16[96,512]{1,0:T(8,128)(2,1)S(1)}, bf16[96,512]{1,0:T(8,128)(2,1)S(1)}, u32[]{:S(2)}, u32[]{:S(2)}) collective-permute-start(bf16[96,512]{1,0:T(8,128)(2,1)S(1)} %fusion.60), channel_id=1, source_target_pairs={{0,16},{2,18},{4,20},{6,22},{8,24},{10,26},{12,28},{14,30},{16,0},... | collective-permute-start | bytes 294920 | tf_op jit(solution)/shard_map/ppermute | solution.py:303
  337.5 7.6 %collective-permute-start.15 = (bf16[192,512]{1,0:T(8,128)(2,1)S(1)}, bf16[192,512]{1,0:T(8,128)(2,1)S(1)}, u32[]{:S(2)}, u32[]{:S(2)}) collective-permute-start(bf16[192,512]{1,0:T(8,128)(2,1)S(1)} %pad_maximum_fusion.13), channel_id=1, source_target_pairs={{0,8},{2,10},{4,12},{6,14},{8,0},{10,2},{12,4},{14,6},{16,24},{18,... | collective-permute-start | bytes 589832 | tf_op jit(solution)/shard_map/ppermute | solution.py:303
  342.7 8.3 %collective-permute-start.23 = (bf16[192,512]{1,0:T(8,128)(2,1)S(1)}, bf16[192,512]{1,0:T(8,128)(2,1)S(1)}, u32[]{:S(2)}, u32[]{:S(2)}) collective-permute-start(bf16[192,512]{1,0:T(8,128)(2,1)S(1)} %pad_maximum_fusion.14), channel_id=1, source_target_pairs={{0,4},{2,6},{4,0},{6,2},{8,12},{10,14},{12,8},{14,10},{16,20},{18,... | collective-permute-start | bytes 589832 | tf_op jit(solution)/shard_map/ppermute | solution.py:303
  345.2 89.5 %collective-permute-start.16 = (bf16[384,512]{1,0:T(8,128)(2,1)S(1)}, bf16[384,512]{1,0:T(8,128)(2,1)S(1)}, u32[]{:S(2)}, u32[]{:S(2)}) collective-permute-start(bf16[384,512]{1,0:T(8,128)(2,1)S(1)} %pad_maximum_fusion.8), channel_id=1, source_target_pairs={{0,4},{2,6},{4,0},{6,2},{8,12},{10,14},{12,8},{14,10},{16,20},{18,... | collective-permute-start | bytes 1179656 | tf_op jit(solution)/shard_map/ppermute | solution.py:303
  351.1 84.0 %collective-permute-start.24 = (bf16[384,512]{1,0:T(8,128)(2,1)S(1)}, bf16[384,512]{1,0:T(8,128)(2,1)S(1)}, u32[]{:S(2)}, u32[]{:S(2)}) collective-permute-start(bf16[384,512]{1,0:T(8,128)(2,1)S(1)} %pad_maximum_fusion.9), channel_id=1, source_target_pairs={{0,8},{2,10},{4,12},{6,14},{8,0},{10,2},{12,4},{14,6},{16,24},{18,... | collective-permute-start | bytes 1179656 | tf_op jit(solution)/shard_map/ppermute | solution.py:303
  434.9 7.3 %collective-permute-start.17 = (bf16[768,512]{1,0:T(8,128)(2,1)S(1)}, bf16[768,512]{1,0:T(8,128)(2,1)S(1)}, u32[]{:S(2)}, u32[]{:S(2)}) collective-permute-start(bf16[768,512]{1,0:T(8,128)(2,1)S(1)} %pad_maximum_fusion.5), channel_id=1, source_target_pairs={{0,2},{2,0},{4,6},{6,4},{8,10},{10,8},{12,14},{14,12},{16,18},{18,... | collective-permute-start | bytes 2359304 | tf_op jit(solution)/shard_map/ppermute | solution.py:303
  435.2 7.3 %collective-permute-start.25 = (bf16[768,512]{1,0:T(8,128)(2,1)S(1)}, bf16[768,512]{1,0:T(8,128)(2,1)S(1)}, u32[]{:S(2)}, u32[]{:S(2)}) collective-permute-start(bf16[768,512]{1,0:T(8,128)(2,1)S(1)} %pad_maximum_fusion.6), channel_id=1, source_target_pairs={{0,2},{2,0},{4,6},{6,4},{8,10},{10,8},{12,14},{14,12},{16,18},{18,... | collective-permute-start | bytes 2359304 | tf_op jit(solution)/shard_map/ppermute | solution.py:303
  (31 other events, 76.3 us)
Sparse Core Ops, SparseCore 0:
  239.7 190.0 all-reduce.2
